TPU v7x, 128 devices: a whole 4x4x4 slice. The times are simulated.
128 devices in a mesh: grp: 2 (over core), row: 16 (over y, x), col: 4 (over z).
Axes of the slice: x: 4, y: 4, z: 4, core: 2. Of those that a mesh axis runs over, the one named last changes fastest.
Arguments:
- root_inverse: bfloat16 [12288, 12288], P(('grp', 'row'), 'col'), may hold values from -0.0546875 to 0.0546875
- child_inverse: bfloat16 [2, 8192, 8192], P('grp', 'row', 'col'), may hold values from -0.0625 to 0.0625
- coupling: bfloat16 [2, 1536, 8192], P('grp', 'col', 'row'), may hold values from -0.0625 to 0.0625
- child_weights: bfloat16 [2, 8192], P('grp', 'col'), may hold values from 0.5 to 2
- root_weights: bfloat16 [12288], P('col'), may hold values from 0.5 to 2
- parent_blocks: int32 [2, 12], replicated, may hold values from 0 to 95, as said below
Outputs:
- grad_root: bfloat16 [12288, 12288], P(('grp', 'row'), 'col')
- grad_child: bfloat16 [2, 8192, 8192], P('grp', 'row', 'col')
- grad_coupling: bfloat16 [2, 1536, 8192], P('grp', 'col', 'row')
Inputs may be any that keep to these rules, and one draw needn't show every extreme that they name: `parent_blocks`: within one child the 12 blocks are distinct; child 0 always names block 0 and block 12288 // 128 - 1; the two children may share blocks.
All inputs are finite; a program needn't handle non-finite values.
Results may differ from a plain program's by a relative error of at most 0.0059.
Values may be sent and summed in bfloat16 or wider, within the bound.
A program may use at most 128 MiB of HBM per device.

v0:
```python
import jax
import jax.numpy as jnp
from jax import lax
from jax.sharding import PartitionSpec as P

BW = 128


def local(root_inverse, child_inverse, coupling, child_weights, root_weights, parent_blocks):
    col_index = lax.axis_index("col")
    col_count = lax.axis_size("col")
    root_rows, root_cols = root_inverse.shape
    local_blocks = root_cols // BW
    share_cols = coupling.shape[1]
    width = share_cols * col_count
    block_count = width // BW
    highest = lax.Precision.HIGHEST
    offset = parent_blocks - col_index * local_blocks
    block_ids = jnp.arange(local_blocks, dtype=jnp.int32)
    owners = [
        (offset[child][:, None] == block_ids[None, :]).astype(jnp.float32) for child in range(2)
    ]
    root_blocks = root_inverse.astype(jnp.float32).reshape(root_rows, local_blocks, BW)
    picks = []
    for child in range(2):
        taken = jnp.einsum("rkb,jk->rjb", root_blocks, owners[child], precision=highest)
        picks.append(taken.reshape(root_rows, width))
    picked = jnp.stack(picks, axis=1)
    selected = lax.psum(picked.astype(jnp.bfloat16), "col")
    mine = lax.dynamic_slice_in_dim(selected, col_index * share_cols, share_cols, 2)
    margin_part = jnp.concatenate(
        [
            jnp.dot(selected[:, child, :].T, mine[:, child, :], preferred_element_type=jnp.float32)
            for child in range(2)
        ],
        axis=0,
    )
    margin = lax.psum_scatter(margin_part, ("grp", "row"), scatter_dimension=0, tiled=True).astype(
        jnp.bfloat16
    )
    factor = child_inverse[0]
    links = coupling[0]
    weights = child_weights[0].astype(jnp.float32)
    links_all = lax.all_gather(links, "col", axis=0, tiled=True)
    solved = lax.psum_scatter(
        jnp.dot(links_all, factor, preferred_element_type=jnp.float32),
        "row",
        scatter_dimension=0,
        tiled=True,
    ).astype(jnp.bfloat16)
    solved_all = lax.all_gather(solved, "row", axis=0, tiled=True)
    scaled = (solved.astype(jnp.float32) * weights[None, :]).astype(jnp.bfloat16)
    adjoint_t = lax.psum_scatter(
        jnp.dot(solved_all, scaled.T, preferred_element_type=jnp.float32),
        "col",
        scatter_dimension=0,
        tiled=True,
    ).astype(jnp.bfloat16)
    adjoint_cols = lax.all_gather(adjoint_t, ("grp", "row"), axis=1, tiled=True).reshape(
        share_cols, 2, width
    )
    lifted = jnp.stack(
        [
            jnp.dot(
                selected[:, child, :],
                adjoint_cols[:, child, :].T,
                preferred_element_type=jnp.float32,
            )
            for child in range(2)
        ],
        axis=1,
    ).astype(jnp.bfloat16)
    lifted_all = lax.all_gather(lifted, "col", axis=2, tiled=True).reshape(
        root_rows, 2, block_count, BW
    )
    placed = jnp.zeros((root_rows, local_blocks, BW), jnp.float32)
    for child in range(2):
        spread = lifted_all[:, child].astype(jnp.float32)
        placed = placed + jnp.einsum("rjb,jk->rkb", spread, owners[child], precision=highest)
    placed = placed.reshape(root_rows, root_cols)
    root_scale = root_weights.astype(jnp.float32)[None, :]
    grad_root = (2.0 * root_inverse.astype(jnp.float32) * root_scale + 2.0 * placed).astype(
        jnp.bfloat16
    )
    margin_row = lax.all_gather(margin, "col", axis=1, tiled=True)
    pulled = (
        2.0 * jnp.dot(margin_row, solved_all, preferred_element_type=jnp.float32) * weights[None, :]
    ).astype(jnp.bfloat16)
    pulled_all = lax.all_gather(pulled, "row", axis=0, tiled=True)
    grad_links = lax.psum_scatter(
        jnp.dot(pulled_all, factor.T, preferred_element_type=jnp.float32),
        "col",
        scatter_dimension=0,
        tiled=True,
    ).astype(jnp.bfloat16)
    grad_factor = jnp.dot(links_all.T, pulled_all, preferred_element_type=jnp.float32)
    grad_factor = (grad_factor + 2.0 * factor.astype(jnp.float32) * weights[None, :]).astype(
        jnp.bfloat16
    )
    return (grad_root, grad_factor[None], grad_links[None])


def solution(mesh):
    return jax.shard_map(
        local,
        mesh=mesh,
        in_specs=(
            P(("grp", "row"), "col"),
            P("grp", "row", "col"),
            P("grp", "col", "row"),
            P("grp", "col"),
            P("col"),
            P(),
        ),
        out_specs=(P(("grp", "row"), "col"), P("grp", "row", "col"), P("grp", "col", "row")),
        check_vma=False,
    )
```

profile of v0, /device:TPU:1, one launch (start us, length us, event | category | flops | bytes accessed | tf_op | source)
XLA Modules:
  0.0 578.5 jit_solution(17137444513439801942)
XLA Ops:
  7.2 0.0 all-gather.15.cloned.1.call-start
  7.2 0.7 all-gather.15.cloned.1.call-update
  7.9 0.0 reduce-scatter.5.cloned.1.call-start
  7.9 31.4 %all-gather.15.cloned.1.call-done = bf16[1,1536,512]{2,1,0:T(8,128)(2,1)} async-done(((bf16[1,384,512]{2,1,0:T(8,128)(2,1)}), bf16[1,1536,512]{2,1,0:T(8,128)(2,1)}) %all-gather.15.cloned.1.call-update) | async-done | bytes 1572880 | tf_op jit(solution)/shard_map/all_gather | solution.py:44
  39.4 10.0 %fusion.6 = f32[1536,2048]{1,0:T(8,128)} fusion(bf16[1,512,2048]{2,1,0:T(8,128)(2,1)} %param.7, bf16[1,1536,512]{2,1,0:T(8,128)(2,1)} %all-gather.15.cloned.1.call-done), kind=kOutput, calls=%fused_computation.12 | convolution fusion | flops 3221225472 | bytes 16252928 | tf_op jit(solution)/shard_map/dot_general | solution.py:46
  49.4 0.0 reduce-scatter.5.cloned.1.call-update
  49.4 0.0 all-gather.7.cloned.1.call-start
  49.5 94.5 %reduce-scatter.5.cloned.1.call-done = f32[96,2048]{1,0:T(8,128)} async-done(((f32[1536,2048]{1,0:T(8,128)}), f32[96,2048]{1,0:T(8,128)}) %reduce-scatter.5.cloned.1.call-update) | async-done | bytes 786448 | tf_op jit(solution)/shard_map/reduce_scatter | solution.py:45
  144.0 1.9 convert_element_type.47
  145.9 0.0 all-gather.7.cloned.1.call-update
  145.9 0.0 all-reduce.2.cloned.1.call-start
  146.0 2.2 copy.20
  148.3 0.6 copy-done.9
  148.8 1.8 fusion.13
  150.6 2.1 copy.11
  152.8 1.8 fusion.14
  154.6 2.2 copy.12
  156.7 1.7 pad_maximum_fusion.1
  158.4 0.0 all-reduce.2.cloned.1.call-update
  158.4 0.0 reduce-scatter.7.cloned.1.call-start
  158.5 0.6 copy-done.7
  159.1 48.1 %all-gather.7.cloned.1.call-done = bf16[1536,2048]{1,0:T(8,128)(2,1)} async-done(((bf16[96,2048]{1,0:T(8,128)(2,1)}), bf16[1536,2048]{1,0:T(8,128)(2,1)}) %all-gather.7.cloned.1.call-update) | async-done | bytes 6291472 | tf_op jit(solution)/shard_map/all_gather | solution.py:51
  207.2 5.7 fusion.19
  212.9 0.0 reduce-scatter.7.cloned.1.call-update
  212.9 0.0 reduce-scatter.9.cloned.1.call-start
  213.0 60.0 %all-reduce.2.cloned.1.call-done = bf16[384,2,1536]{0,2,1:T(8,128)(2,1)} async-done(((bf16[384,2,1536]{0,2,1:T(8,128)(2,1)}), bf16[384,2,1536]{0,2,1:T(8,128)(2,1)}) %all-reduce.2.cloned.1.call-update) | async-done | bytes 2359312 | tf_op jit(solution)/shard_map/psum | solution.py:29
  273.0 2.4 fusion.17
  275.4 0.9 fusion.18
  276.3 2.5 pad_maximum_fusion
  278.8 0.0 reduce-scatter.9.cloned.1.call-update
  278.8 0.0 all-gather.9.cloned.1.call-start
  278.9 16.9 %reduce-scatter.7.cloned.1.call-done = f32[384,96]{0,1:T(8,128)} async-done(((f32[1536,96]{0,1:T(8,128)}), f32[384,96]{0,1:T(8,128)}) %reduce-scatter.7.cloned.1.call-update) | async-done | bytes 147472 | tf_op jit(solution)/shard_map/reduce_scatter | solution.py:53
  295.8 1.6 convert_element_type.50
  297.4 0.0 all-gather.9.cloned.1.call-update
  297.4 0.0 all-gather.13.cloned.1.call-start
  297.5 85.5 %reduce-scatter.9.cloned.1.call-done = f32[96,384]{1,0:T(8,128)} async-done(((f32[3072,384]{1,0:T(8,128)}), f32[96,384]{1,0:T(8,128)}) %reduce-scatter.9.cloned.1.call-update) | async-done | bytes 147472 | tf_op jit(solution)/shard_map/reduce_scatter | solution.py:38
  383.0 0.9 convert_element_type.52
  383.9 10.0 %all_gather.22 = bf16[96,1536]{1,0:T(8,128)(2,1)S(1)} all-gather(bf16[96,384]{1,0:T(8,128)(2,1)S(1)} %convert_element_type.52), channel_id=1, replica_groups=mesh['grp'=2,'row'=16,'col'=4] {'col'}, dimensions={1}, use_global_device_ids=true | all-gather | bytes 368640 | tf_op jit(solution)/shard_map/all_gather | solution.py:85
  394.0 4.7 fusion.3
  398.7 0.0 all-gather.13.cloned.1.call-update
  398.7 0.2 all-gather.11.cloned.1.call-start
  399.0 32.1 %all-gather.9.cloned.1.call-done = bf16[384,3072]{0,1:T(8,128)(2,1)} async-done(((bf16[384,96]{0,1:T(8,128)(2,1)}), bf16[384,3072]{0,1:T(8,128)(2,1)}) %all-gather.9.cloned.1.call-update) | async-done | bytes 2359312 | tf_op jit(solution)/shard_map/all_gather | solution.py:59
  431.0 2.2 fusion.15
  433.3 0.8 fusion.16
  434.1 0.9 pad_maximum_fusion.2
  435.0 0.0 reduce-scatter.11.cloned.1.call-start
  435.0 58.7 %all-gather.13.cloned.1.call-done = bf16[1536,2048]{1,0:T(8,128)(2,1)} async-done(((bf16[96,2048]{1,0:T(8,128)(2,1)}), bf16[1536,2048]{1,0:T(8,128)(2,1)}) %all-gather.13.cloned.1.call-update) | async-done | bytes 6291472 | tf_op jit(solution)/shard_map/all_gather | solution.py:89
  493.8 8.6 %fusion.4 = f32[1536,512]{1,0:T(8,128)} fusion(bf16[1536,2048]{1,0:T(8,128)(2,1)} %all-gather.13.cloned.1.call-done, bf16[1,512,2048]{2,1,0:T(8,128)(2,1)} %param.7), kind=kOutput, calls=%fused_computation.10 | convolution fusion | flops 3221225472 | bytes 11534336 | tf_op jit(solution)/shard_map/dot_general | solution.py:91
  502.4 0.0 reduce-scatter.11.cloned.1.call-update
  502.4 1.6 copy-done.3
  504.0 2.5 copy.13
  506.5 22.5 %all-gather.11.cloned.1.call-done = bf16[384,2,1536]{2,0,1:T(8,128)(2,1)} async-done(((bf16[384,2,384]{2,0,1:T(8,128)(2,1)}), bf16[384,2,1536]{2,0,1:T(8,128)(2,1)}) %all-gather.11.cloned.1.call-update) | async-done | bytes 2359312 | tf_op jit(solution)/shard_map/all_gather | solution.py:73
  528.9 3.0 copy.14
  532.0 1.3 fusion.33
  533.3 1.4 copy.18
  534.7 2.3 copy.19
  537.0 0.9 fusion.9
  537.9 0.9 add_multiply_fusion
  538.9 1.1 copy-done
  540.0 2.9 fusion
  542.9 3.7 fusion.2
  546.6 2.4 copy.17
  549.0 20.8 %reduce-scatter.11.cloned.1.call-done = f32[384,512]{1,0:T(8,128)} async-done(((f32[1536,512]{1,0:T(8,128)}), f32[384,512]{1,0:T(8,128)}) %reduce-scatter.11.cloned.1.call-update) | async-done | bytes 786448 | tf_op jit(solution)/shard_map/reduce_scatter | solution.py:90
  569.7 1.9 convert_bitcast_fusion
  (35 shorter events, 0.1 us)
Async XLA Ops:
  7.2 32.2 %all-gather.15.cloned.1.call-start = ((), (), s32[]{:S(2)}) async-start(), calls=%async_computation.13 | async-start | bytes 1966080 | tf_op jit(solution)/shard_map/all_gather | solution.py:44
  7.9 136.1 %reduce-scatter.5.cloned.1.call-start = ((), (), s32[]{:S(2)}) async-start(), calls=%async_computation.5 | async-start | bytes 13369344 | tf_op jit(solution)/shard_map/reduce_scatter | solution.py:45
  49.4 157.8 %all-gather.7.cloned.1.call-start = ((), (), s32[]{:S(2)}) async-start(), calls=%async_computation.6 | async-start | bytes 6684672 | tf_op jit(solution)/shard_map/all_gather | solution.py:51
  145.9 127.1 %all-reduce.2.cloned.1.call-start = ((), (), s32[]{:S(2)}) async-start(), calls=%async_computation.4 | async-start | bytes 4718592 | tf_op jit(solution)/shard_map/psum | solution.py:29
  146.0 2.3 copy-start.11
  148.3 0.6 copy-start.9
  158.4 0.7 copy-start.7
  158.4 48.8 %copy-start.1 = (bf16[96,2048]{1,0:T(8,128)(2,1)S(1)}, bf16[96,2048]{1,0:T(8,128)(2,1)}, u32[]{:S(2)}) copy-start(bf16[96,2048]{1,0:T(8,128)(2,1)} %convert_element_type.47) | copy-start | bytes 1179652
  158.4 137.4 %reduce-scatter.7.cloned.1.call-start = ((), (), s32[]{:S(2)}) async-start(), calls=%async_computation.7 | async-start | bytes 737280 | tf_op jit(solution)/shard_map/reduce_scatter | solution.py:53
  212.9 170.1 %reduce-scatter.9.cloned.1.call-start = ((), (), s32[]{:S(2)}) async-start(), calls=%async_computation.10 | async-start | bytes 4866048 | tf_op jit(solution)/shard_map/reduce_scatter | solution.py:38
  273.0 2.4 copy-start.2
  278.8 152.2 %all-gather.9.cloned.1.call-start = ((), (), s32[]{:S(2)}) async-start(), calls=%async_computation.8 | async-start | bytes 2433024 | tf_op jit(solution)/shard_map/all_gather | solution.py:59
  297.4 196.4 %all-gather.13.cloned.1.call-start = ((), (), s32[]{:S(2)}) async-start(), calls=%async_computation.11 | async-start | bytes 6684672 | tf_op jit(solution)/shard_map/all_gather | solution.py:89
  297.5 101.2 %copy-start.5 = (f32[2048]{0:T(1024)}, f32[2048]{0:T(1024)S(1)}, u32[]{:S(2)}) copy-start(f32[2048]{0:T(1024)S(1)} %broadcast_multiply_fusion) | copy-start | bytes 24580
  398.7 130.2 %all-gather.11.cloned.1.call-start = ((), (), s32[]{:S(2)}) async-start(), calls=%async_computation.9 | async-start | bytes 2949120 | tf_op jit(solution)/shard_map/all_gather | solution.py:73
  431.0 2.2 copy-start.12
  435.0 134.8 %reduce-scatter.11.cloned.1.call-start = ((), (), s32[]{:S(2)}) async-start(), calls=%async_computation.12 | async-start | bytes 3932160 | tf_op jit(solution)/shard_map/reduce_scatter | solution.py:90
  502.4 1.6 copy-start.3
  504.0 2.5 copy-start.8
  534.7 2.3 copy-start.10
  537.0 5.8 %slice-start = ((s8[6291456]{0:T(1024)(128)(4,1)}), s8[4194304]{0:T(1024)(128)(4,1)S(1)}, s32[]{:S(2)}) async-start(s8[6291456]{0:T(1024)(128)(4,1)} %bitcast.102), calls=%async_computation.14 | async-start | bytes 8388608
  537.9 2.0 copy-start
  537.9 4.9 slice-start.1
  539.9 2.9 copy-start.4
  539.9 2.9 copy-start.6
  540.0 2.9 copy-start.13
Sparse Core Ops, SparseCore 0:
  9.6 29.7 all-gather.14
  49.5 94.3 reduce-scatter.4
  146.7 60.5 all-gather.6
  210.0 62.8 all-reduce.1
  275.8 19.9 reduce-scatter.6
  299.4 83.5 reduce-scatter.8
  385.8 45.1 all-gather.8
  433.7 59.9 all-gather.12
  496.0 32.8 all-gather.10
  531.2 38.4 reduce-scatter.10
where the time goes:
time: 579 us
  waiting for transfers between devices  471 us (81%)
  matrix products  44.4 us (8%)
  local copies, waits for them, and re-layouts  23.3 us (4%)
  between operations  14.4 us (2%)
  other arithmetic  14.3 us (2%)
  blocking collectives  10 us (2%)
    reduce_scatter x1, waiting for transfers between devices, local(): lax.psum_scatter(jnp.dot(links_all, factor, preferred_element_type=jnp.fl...  94.5 us
    reduce_scatter x1, waiting for transfers between devices, local(): lax.psum_scatter(margin_part, ('grp', 'row'), scatter_dimension=0, tiled=...  85.5 us
    psum x1, waiting for transfers between devices, local(): selected = lax.psum(picked.astype(jnp.bfloat16), 'col')  60 us
    all_gather x1, waiting for transfers between devices, local(): pulled_all = lax.all_gather(pulled, 'row', axis=0, tiled=True)  58.7 us
    all_gather x1, waiting for transfers between devices, local(): solved_all = lax.all_gather(solved, 'row', axis=0, tiled=True)  48.1 us
    all_gather x1, waiting for transfers between devices, local(): lax.all_gather(adjoint_t, ('grp', 'row'), axis=1, tiled=True)  32.1 us
    all_gather x1, waiting for transfers between devices, local(): links_all = lax.all_gather(links, 'col', axis=0, tiled=True)  31.4 us
    all_gather x1, waiting for transfers between devices, local(): lax.all_gather(lifted, 'col', axis=2, tiled=True)  22.5 us
  transfers between devices with their start and end apart: 10, of which 10 were waited for; matrix products, arithmetic and copies ran while one was open for 11% of the time, Pallas kernels for 0%

commit v1 on v0

--- a/solution.py
+++ b/solution.py
@@ -4,6 +4,16 @@
 from jax.sharding import PartitionSpec as P
 
 BW = 128
+
+
+def map_columns(obj, dimension_no):
+    obj = jnp.moveaxis(obj, 0, dimension_no)
+    local_part = obj.shape
+    return obj.reshape(
+        *local_part[:dimension_no],
+        local_part[dimension_no] * local_part[dimension_no + 1],
+        *local_part[dimension_no + 2 :]
+    )
 
 
 def local(root_inverse, child_inverse, coupling, child_weights, root_weights, parent_blocks):
@@ -41,7 +51,21 @@
     factor = child_inverse[0]
     links = coupling[0]
     weights = child_weights[0].astype(jnp.float32)
-    links_all = lax.all_gather(links, "col", axis=0, tiled=True)
+    n_parts = lax.axis_size("col")
+    queue = [(p, (p + 1) % n_parts) for p in range(n_parts)]
+    made = [(i, src_i) for src_i, i in queue]
+    i0 = 0
+    k_now, f_next = ([], [])
+    while i0 < n_parts - 1:
+        if i0 % 2 == 0:
+            k_now.append(lax.ppermute(k_now[-1] if k_now else links, "col", queue))
+        else:
+            f_next.append(lax.ppermute(f_next[-1] if f_next else links, "col", made))
+        i0 = i0 + 1
+    m_next = jnp.stack([*k_now[::-1], links, *f_next])
+    y2 = lax.axis_index("col") - len(k_now)
+    m_next = m_next[(jnp.arange(n_parts) - y2) % n_parts]
+    links_all = map_columns(m_next, 0)
     solved = lax.psum_scatter(
         jnp.dot(links_all, factor, preferred_element_type=jnp.float32),
         "row",

time: 579 us -> 521 us (0.90)
  waiting for transfers between devices: 471 us -> 410 us
    psum x1, waiting for transfers between devices: 60 us -> 7.29 us  [local(): selected = lax.psum(picked.astype(jnp.bfloat16), 'col')]
    all_gather x1 -> x0, waiting for transfers between devices: 31.4 us -> none  [local(): links_all = lax.all_gather(links, 'col', axis=0, tiled=True)]
    ppermute x0 -> x3, waiting for transfers between devices: none -> 19.5 us  [the longest x2 19.5 us: local(): k_now.append(lax.ppermute(k_now[-1] if k_now else links, 'col', queue))]
    unnamed x37 -> x27, local copies, waits for them, and re-layouts: 14.7 us -> 9.86 us
  transfers between devices with their start and end apart: 10 -> 12, of which waited for: 10 -> 11; matrix products, arithmetic and copies ran while one was open for 11% -> 12% of each run, Pallas kernels for 0% -> 0%
where the time goes in v1:
time: 521 us; the launch traced here: 520 us
  waiting for transfers between devices  410 us (79%)
  matrix products  43.8 us (8%)
  local copies, waits for them, and re-layouts  19.5 us (4%)
  between operations  15.8 us (3%)
  other arithmetic  15.6 us (3%)
  blocking collectives  10 us (2%)
  starting transfers between devices  5.3 us (1%)
    reduce_scatter x1, waiting for transfers between devices, local(): lax.psum_scatter(jnp.dot(links_all, factor, preferred_element_type=jnp.fl...  94.8 us
    reduce_scatter x1, waiting for transfers between devices, local(): lax.psum_scatter(margin_part, ('grp', 'row'), scatter_dimension=0, tiled=...  86.3 us
    all_gather x1, waiting for transfers between devices, local(): pulled_all = lax.all_gather(pulled, 'row', axis=0, tiled=True)  58.6 us
    all_gather x1, waiting for transfers between devices, local(): solved_all = lax.all_gather(solved, 'row', axis=0, tiled=True)  48.7 us
    all_gather x1, waiting for transfers between devices, local(): lax.all_gather(adjoint_t, ('grp', 'row'), axis=1, tiled=True)  32.1 us
    all_gather x1, waiting for transfers between devices, local(): lax.all_gather(lifted, 'col', axis=2, tiled=True)  25.8 us
    reduce_scatter x1, waiting for transfers between devices, local(): lax.psum_scatter(jnp.dot(pulled_all, factor.T, preferred_element_type=jnp...  20.4 us
    ppermute x2, waiting for transfers between devices, local(): k_now.append(lax.ppermute(k_now[-1] if k_now else links, 'col', queue))  19.5 us
  transfers between devices with their start and end apart: 12, of which 11 were waited for; matrix products, arithmetic and copies ran while one was open for 12% of the time, Pallas kernels for 0%

profile of v1, /device:TPU:1, one launch (start us, length us, event | category | flops | bytes accessed | tf_op | source)
XLA Modules:
  0.0 519.9 jit_solution(13768307647754515620)
XLA Ops:
  8.0 0.0 reduce-scatter.5.cloned.1.call-start
  8.0 2.5 collective-permute-start
  10.6 2.2 collective-permute-start.2
  12.8 8.9 %collective-permute-done = bf16[384,512]{1,0:T(8,128)(2,1)S(1)} collective-permute-done((bf16[384,512]{1,0:T(8,128)(2,1)}, bf16[384,512]{1,0:T(8,128)(2,1)S(1)}, u32[]{:S(2)}, u32[]{:S(2)}) %collective-permute-start) | collective-permute-done | bytes 393248 | tf_op jit(solution)/shard_map/ppermute | solution.py:61
  21.8 10.6 %collective-permute-done.1 = bf16[384,512]{1,0:T(8,128)(2,1)S(1)} collective-permute-done((bf16[384,512]{1,0:T(8,128)(2,1)S(1)}, bf16[384,512]{1,0:T(8,128)(2,1)S(1)}, u32[]{:S(2)}, u32[]{:S(2)}) %collective-permute-start.1) | collective-permute-done | bytes 393248 | tf_op jit(solution)/shard_map/ppermute | solution.py:61
  32.4 1.2 pad_maximum_fusion.2
  33.5 0.6 gather_fusion
  34.2 8.5 %fusion.5 = f32[1536,2048]{1,0:T(8,128)} fusion(bf16[1536,512]{1,0:T(8,128)(2,1)S(1)} %bitcast.96, bf16[1,512,2048]{2,1,0:T(8,128)(2,1)} %param.7), kind=kOutput, calls=%fused_computation.12 | convolution fusion | flops 3221225472 | bytes 16252928 | tf_op jit(solution)/shard_map/dot_general | solution.py:70
  42.7 0.0 reduce-scatter.5.cloned.1.call-update
  42.7 0.0 all-gather.5.cloned.1.call-start
  42.8 94.8 %reduce-scatter.5.cloned.1.call-done = f32[96,2048]{1,0:T(8,128)} async-done(((f32[1536,2048]{1,0:T(8,128)}), f32[96,2048]{1,0:T(8,128)}) %reduce-scatter.5.cloned.1.call-update) | async-done | bytes 786448 | tf_op jit(solution)/shard_map/reduce_scatter | solution.py:69
  137.5 1.9 convert_element_type.47
  139.5 0.0 all-reduce.2.cloned.1.call-start
  139.6 2.2 copy.16
  141.8 1.8 fusion.10
  143.6 2.1 copy.9
  145.8 1.8 fusion.11
  147.6 2.1 copy.10
  149.7 1.7 pad_maximum_fusion.1
  151.4 0.0 all-reduce.2.cloned.1.call-update
  151.4 0.0 reduce-scatter.7.cloned.1.call-start
  151.5 0.6 copy-done.5
  152.1 48.7 %all-gather.5.cloned.1.call-done = bf16[1536,2048]{1,0:T(8,128)(2,1)} async-done(((bf16[96,2048]{1,0:T(8,128)(2,1)}), bf16[1536,2048]{1,0:T(8,128)(2,1)}) %all-gather.5.cloned.1.call-update) | async-done | bytes 6291472 | tf_op jit(solution)/shard_map/all_gather | solution.py:75
  200.8 5.7 %fusion.16 = f32[1536,96]{0,1:T(8,128)} fusion(bf16[1536,2048]{1,0:T(8,128)(2,1)} %all-gather.5.cloned.1.call-done, bf16[96,2048]{1,0:T(8,128)(2,1)S(1)} %copy-done.1, f32[2048]{0:T(1024)S(1)} %bitcast.103), kind=kOutput, calls=%fused_computation.34 | convolution fusion | flops 604569600 | bytes 7282688 | tf_op jit(solution)/shard_map/dot_general | solution.py:78
  206.5 0.0 reduce-scatter.7.cloned.1.call-update
  206.5 0.0 reduce-scatter.9.cloned.1.call-start
  206.5 7.3 %all-reduce.2.cloned.1.call-done = bf16[384,2,1536]{0,2,1:T(8,128)(2,1)} async-done(((bf16[384,2,1536]{0,2,1:T(8,128)(2,1)}), bf16[384,2,1536]{0,2,1:T(8,128)(2,1)}) %all-reduce.2.cloned.1.call-update) | async-done | bytes 2359312 | tf_op jit(solution)/shard_map/psum | solution.py:39
  213.8 2.4 fusion.14
  216.2 0.9 fusion.15
  217.1 2.5 pad_maximum_fusion
  219.7 0.0 reduce-scatter.9.cloned.1.call-update
  219.7 0.0 all-gather.7.cloned.1.call-start
  219.7 16.4 %reduce-scatter.7.cloned.1.call-done = f32[384,96]{0,1:T(8,128)} async-done(((f32[1536,96]{0,1:T(8,128)}), f32[384,96]{0,1:T(8,128)}) %reduce-scatter.7.cloned.1.call-update) | async-done | bytes 147472 | tf_op jit(solution)/shard_map/reduce_scatter | solution.py:77
  236.2 1.6 convert_element_type.50
  237.7 0.0 all-gather.7.cloned.1.call-update
  237.8 0.0 all-gather.11.cloned.1.call-start
  237.8 86.3 %reduce-scatter.9.cloned.1.call-done = f32[96,384]{1,0:T(8,128)} async-done(((f32[3072,384]{1,0:T(8,128)}), f32[96,384]{1,0:T(8,128)}) %reduce-scatter.9.cloned.1.call-update) | async-done | bytes 147472 | tf_op jit(solution)/shard_map/reduce_scatter | solution.py:48
  324.1 0.9 convert_element_type.52
  325.0 10.0 %all_gather.18 = bf16[96,1536]{1,0:T(8,128)(2,1)S(1)} all-gather(bf16[96,384]{1,0:T(8,128)(2,1)S(1)} %convert_element_type.52), channel_id=1, replica_groups=mesh['grp'=2,'row'=16,'col'=4] {'col'}, dimensions={1}, use_global_device_ids=true | all-gather | bytes 368640 | tf_op jit(solution)/shard_map/all_gather | solution.py:109
  335.0 4.7 fusion.2
  339.8 0.0 all-gather.11.cloned.1.call-update
  339.8 0.2 all-gather.9.cloned.1.call-start
  340.0 32.1 %all-gather.7.cloned.1.call-done = bf16[384,3072]{0,1:T(8,128)(2,1)} async-done(((bf16[384,96]{0,1:T(8,128)(2,1)}), bf16[384,3072]{0,1:T(8,128)(2,1)}) %all-gather.7.cloned.1.call-update) | async-done | bytes 2359312 | tf_op jit(solution)/shard_map/all_gather | solution.py:83
  372.1 2.2 fusion.13
  374.3 0.8 fusion.12
  375.1 0.9 pad_maximum_fusion.3
  376.0 0.0 all-gather.9.cloned.1.call-update
  376.0 0.0 reduce-scatter.11.cloned.1.call-start
  376.1 58.6 %all-gather.11.cloned.1.call-done = bf16[1536,2048]{1,0:T(8,128)(2,1)} async-done(((bf16[96,2048]{1,0:T(8,128)(2,1)}), bf16[1536,2048]{1,0:T(8,128)(2,1)}) %all-gather.11.cloned.1.call-update) | async-done | bytes 6291472 | tf_op jit(solution)/shard_map/all_gather | solution.py:113
  434.7 8.6 %fusion.3 = f32[1536,512]{1,0:T(8,128)} fusion(bf16[1536,2048]{1,0:T(8,128)(2,1)} %all-gather.11.cloned.1.call-done, bf16[1,512,2048]{2,1,0:T(8,128)(2,1)} %param.7), kind=kOutput, calls=%fused_computation.10 | convolution fusion | flops 3221225472 | bytes 11534336 | tf_op jit(solution)/shard_map/dot_general | solution.py:115
  443.3 0.0 reduce-scatter.11.cloned.1.call-update
  443.3 0.7 copy-done.6
  443.9 25.8 %all-gather.9.cloned.1.call-done = bf16[384,2,1536]{2,0,1:T(8,128)(2,1)} async-done(((bf16[384,2,384]{2,0,1:T(8,128)(2,1)}), bf16[384,2,1536]{2,0,1:T(8,128)(2,1)}) %all-gather.9.cloned.1.call-update) | async-done | bytes 2359312 | tf_op jit(solution)/shard_map/all_gather | solution.py:97
  469.7 3.0 copy.11
  472.7 1.7 fusion.32
  474.4 2.3 copy.15
  476.7 2.3 copy.14
  479.1 0.9 fusion.8
  480.0 0.9 add_multiply_fusion
  480.9 1.7 copy-done
  482.6 2.9 fusion
  485.5 4.6 fusion.1
  490.1 20.4 %reduce-scatter.11.cloned.1.call-done = f32[384,512]{1,0:T(8,128)} async-done(((f32[1536,512]{1,0:T(8,128)}), f32[384,512]{1,0:T(8,128)}) %reduce-scatter.11.cloned.1.call-update) | async-done | bytes 786448 | tf_op jit(solution)/shard_map/reduce_scatter | solution.py:114
  510.5 1.9 convert_bitcast_fusion
  (32 shorter events, 0.1 us)
Async XLA Ops:
  8.0 129.5 %reduce-scatter.5.cloned.1.call-start = ((), (), s32[]{:S(2)}) async-start(), calls=%async_computation.5 | async-start | bytes 13369344 | tf_op jit(solution)/shard_map/reduce_scatter | solution.py:69
  8.0 13.7 %collective-permute-start = (bf16[384,512]{1,0:T(8,128)(2,1)}, bf16[384,512]{1,0:T(8,128)(2,1)S(1)}, u32[]{:S(2)}, u32[]{:S(2)}) collective-permute-start(bf16[384,512]{1,0:T(8,128)(2,1)} %bitcast.98), channel_id=1, source_target_pairs={{0,1},{1,2},{2,3},{3,0},{4,5},{5,6},{6,7},{7,4},{8,9},{9,10},{10,1... | collective-permute-start | bytes 1179656 | tf_op jit(solution)/shard_map/ppermute | solution.py:61
  10.6 11.2 %collective-permute-start.2 = (bf16[384,512]{1,0:T(8,128)(2,1)}, bf16[384,512]{1,0:T(8,128)(2,1)S(1)}, u32[]{:S(2)}, u32[]{:S(2)}) collective-permute-start(bf16[384,512]{1,0:T(8,128)(2,1)} %bitcast.99), channel_id=1, source_target_pairs={{1,0},{2,1},{3,2},{0,3},{5,4},{6,5},{7,6},{4,7},{9,8},{10,9},{11,1... | collective-permute-start | bytes 1179656 | tf_op jit(solution)/shard_map/ppermute | solution.py:63
  21.7 10.6 %collective-permute-start.1 = (bf16[384,512]{1,0:T(8,128)(2,1)S(1)}, bf16[384,512]{1,0:T(8,128)(2,1)S(1)}, u32[]{:S(2)}, u32[]{:S(2)}) collective-permute-start(bf16[384,512]{1,0:T(8,128)(2,1)S(1)} %collective-permute-done), channel_id=1, source_target_pairs={{0,1},{1,2},{2,3},{3,0},{4,5},{5,6},{6,7},{7,4},{8,9},{9,10},{10,1... | collective-permute-start | bytes 1179656 | tf_op jit(solution)/shard_map/ppermute | solution.py:61
  34.2 8.5 %copy-start.3 = (bf16[4,384,512]{2,1,0:T(8,128)(2,1)}, bf16[4,384,512]{2,1,0:T(8,128)(2,1)S(1)}, u32[]{:S(2)}) copy-start(bf16[4,384,512]{2,1,0:T(8,128)(2,1)S(1)} %gather_fusion) | copy-start | bytes 4718596
  42.7 158.0 %all-gather.5.cloned.1.call-start = ((), (), s32[]{:S(2)}) async-start(), calls=%async_computation.6 | async-start | bytes 6684672 | tf_op jit(solution)/shard_map/all_gather | solution.py:75
  139.5 74.3 %all-reduce.2.cloned.1.call-start = ((), (), s32[]{:S(2)}) async-start(), calls=%async_computation.4 | async-start | bytes 4718592 | tf_op jit(solution)/shard_map/psum | solution.py:39
  139.5 2.3 copy-start.7
  151.4 0.7 copy-start.5
  151.4 49.4 %copy-start.1 = (bf16[96,2048]{1,0:T(8,128)(2,1)S(1)}, bf16[96,2048]{1,0:T(8,128)(2,1)}, u32[]{:S(2)}) copy-start(bf16[96,2048]{1,0:T(8,128)(2,1)} %convert_element_type.47) | copy-start | bytes 1179652
  151.4 84.8 %reduce-scatter.7.cloned.1.call-start = ((), (), s32[]{:S(2)}) async-start(), calls=%async_computation.7 | async-start | bytes 737280 | tf_op jit(solution)/shard_map/reduce_scatter | solution.py:77
  206.5 117.6 %reduce-scatter.9.cloned.1.call-start = ((), (), s32[]{:S(2)}) async-start(), calls=%async_computation.10 | async-start | bytes 4866048 | tf_op jit(solution)/shard_map/reduce_scatter | solution.py:48
  213.8 2.4 copy-start.2
  219.7 152.4 %all-gather.7.cloned.1.call-start = ((), (), s32[]{:S(2)}) async-start(), calls=%async_computation.8 | async-start | bytes 2433024 | tf_op jit(solution)/shard_map/all_gather | solution.py:83
  237.8 196.9 %all-gather.11.cloned.1.call-start = ((), (), s32[]{:S(2)}) async-start(), calls=%async_computation.11 | async-start | bytes 6684672 | tf_op jit(solution)/shard_map/all_gather | solution.py:113
  339.8 129.9 %all-gather.9.cloned.1.call-start = ((), (), s32[]{:S(2)}) async-start(), calls=%async_computation.9 | async-start | bytes 2949120 | tf_op jit(solution)/shard_map/all_gather | solution.py:97
  372.1 2.2 copy-start.8
  376.0 134.5 %reduce-scatter.11.cloned.1.call-start = ((), (), s32[]{:S(2)}) async-start(), calls=%async_computation.12 | async-start | bytes 3932160 | tf_op jit(solution)/shard_map/reduce_scatter | solution.py:114
  443.3 0.7 copy-start.6
  479.1 6.4 %slice-start = ((s8[6291456]{0:T(1024)(128)(4,1)}), s8[4194304]{0:T(1024)(128)(4,1)S(1)}, s32[]{:S(2)}) async-start(s8[6291456]{0:T(1024)(128)(4,1)} %bitcast.105), calls=%async_computation.13 | async-start | bytes 8388608
  480.0 2.6 copy-start
  480.0 5.5 %slice-start.1 = ((s8[6291456]{0:T(1024)(128)(4,1)}), s8[2097152]{0:T(1024)(128)(4,1)S(1)}, s32[]{:S(2)}) async-start(s8[6291456]{0:T(1024)(128)(4,1)} %bitcast.105), calls=%async_computation.14 | async-start | bytes 4194304
  482.6 2.9 copy-start.4
  482.6 2.9 copy-start.9
Sparse Core Ops, SparseCore 0:
  42.8 94.6 reduce-scatter.4
  140.2 60.4 all-gather.4
Sparse Core Ops, SparseCore 1:
  151.5 62.3 all-reduce.1
  216.7 19.4 reduce-scatter.6
  239.8 84.3 reduce-scatter.8
  326.9 45.1 all-gather.6
  374.8 59.8 all-gather.10
  436.9 32.7 all-gather.8
  472.0 38.5 reduce-scatter.10
